TPU v7x, 256 devices: a whole 4x4x8 slice. The times are simulated.
256 devices in a mesh: shot: 4 (over x_hi, core), space: 64 (over x_lo, y, z).
Axes of the slice: x: 4 (x_hi: 2, x_lo: 2; x = x_hi * 2 + x_lo), y: 4, z: 8, core: 2. Of those that a mesh axis runs over, the one named last changes fastest.
Arguments:
- residual_traces: float32 [4, 12, 16384], P('shot', None, 'space'), may hold values from -6 to 6
- owners: int32 [4, 16384, 1], P('shot', 'space'), may hold values from 0 to 63; in each aligned block of 256 rows (0 to 255, 256 to 511, ..., all dimensions but the last counted through in order) at most 8 rows name the same one
- surface_cells: int32 [4, 16384], P('shot', 'space'), may hold values from 0 to 511
- trace_counts: int32 [4], P('shot'), may hold values from 4096 to 16384, as said below
- start_current: float32 [4, 512, 64, 256], P('shot', 'space'), may hold values from -6 to 6
- start_later: float32 [4, 512, 64, 256], P('shot', 'space'), may hold values from -6 to 6
- forward_accel: bfloat16 [4, 12, 512, 64, 256], P('shot', None, 'space'), may hold values from -6 to 6
- courant_sq: float32 [512, 64, 256], P('space'), may hold values from 0.04 to 0.16
Outputs:
- adjoint_field: float32 [4, 512, 64, 256], P('shot', 'space')
- velocity_grad: float32 [512, 64, 256], P('space', 'shot')
Inputs may be any that keep to these rules, and one draw needn't show every extreme that they name: `owners`: among the receivers of one device, no subdomain is named more than 8 times. `trace_counts`: some shot has all 16384 traces live.
All inputs are finite; a program needn't handle non-finite values.
Results may differ from a plain program's by a relative error of at most 0.0003.
Values sent between devices are 32-bit elements; how exact they have to be, the bound alone decides.
A program may use at most 64 MiB of HBM per device.

v0:
```python
import jax
import jax.numpy as jnp
from jax import lax
from jax.sharding import PartitionSpec as P

STENCIL_WEIGHTS = (-205.0 / 72.0, 8.0 / 5.0, -1.0 / 5.0, 8.0 / 315.0, -1.0 / 560.0)


def extended_2(shard, sides, width):
    for axis, dim in sides:
        size, length = (lax.axis_size(axis), shard.shape[dim])
        up = [(i, (i + 1) % size) for i in range(size - 1)]
        down = [(j, i) for i, j in up]
        last = lax.slice_in_dim(shard, length - width, length, axis=dim)
        leading = lax.slice_in_dim(shard, 0, width, axis=dim)
        before = lax.ppermute(last, axis, up)
        after = lax.ppermute(leading, axis, down)
        shard = jnp.concatenate([before, shard, after], axis=dim)
    return shard


def laplace(padded):
    length = padded.shape[0] - 8
    across = padded.shape[1] - 8
    height = padded.shape[2] - 8

    def window(off_x, off_y, off_z):
        return lax.slice(
            padded,
            (4 + off_x, 4 + off_y, 4 + off_z),
            (4 + off_x + length, 4 + off_y + across, 4 + off_z + height),
        )

    summed = 3.0 * STENCIL_WEIGHTS[0] * window(0, 0, 0)
    for offset in range(1, 5):
        six_taps = window(offset, 0, 0) + window(-offset, 0, 0) + window(0, offset, 0)
        six_taps = six_taps + window(0, -offset, 0) + window(0, 0, offset) + window(0, 0, -offset)
        summed = summed + STENCIL_WEIGHTS[offset] * six_taps
    return summed


def laplace_rim(extended):
    return laplace(jnp.pad(extended, ((0, 0), (4, 4), (4, 4))))


def onehot_cells(targets, plane_cells):
    return (targets[:, None] == jnp.arange(plane_cells, dtype=jnp.int32)[None, :]).astype(
        jnp.float32
    )


def shards(
    residual_traces,
    owners,
    surface_cells,
    trace_counts,
    start_current,
    start_later,
    forward_accel,
    courant_sq,
):
    traces = residual_traces[0]
    owner_row = owners[0, :, 0]
    surface = surface_cells[0]
    live_count = trace_counts[0]
    forward = forward_accel[0]
    first_field = start_current[0]
    prior_field = start_later[0]
    length, across, height = courant_sq.shape
    plane_cells = length * across
    steps_all = traces.shape[0]
    my_index = lax.axis_index("space")
    piece_traces = lax.all_gather(traces, "space", axis=1, tiled=True)
    piece_owner = lax.all_gather(owner_row[None, :], "space", axis=1, tiled=True)
    piece_surface = lax.all_gather(surface[None, :], "space", axis=1, tiled=True)
    number = jnp.arange(piece_traces.shape[1], dtype=jnp.int32)
    keep = (number < live_count) & (piece_owner[0] == my_index)
    targets = jnp.where(keep, piece_surface[0], -1)
    table = onehot_cells(targets, plane_cells)
    planes = jnp.dot(
        piece_traces, table, precision=lax.Precision.HIGHEST, preferred_element_type=jnp.float32
    )
    planes = planes.reshape(steps_all, length, across)
    empty = jnp.zeros((length, across, height), jnp.float32)

    def advance(section, state):
        current, later, gradient = state
        extended = extended_2(current, (("space", 0),), 4)
        fresh = 2.0 * current - later + courant_sq * laplace_rim(extended)
        fresh = fresh.at[:, :, 2].add(lax.dynamic_index_in_dim(planes, section, 0, keepdims=False))
        accel = lax.dynamic_index_in_dim(forward, section, 0, keepdims=False).astype(jnp.float32)
        return (fresh, current, gradient + fresh * accel)

    current, later, gradient = lax.fori_loop(
        0, steps_all, advance, (first_field, prior_field, empty)
    )
    velocity_grad = lax.psum_scatter(gradient, "shot", scatter_dimension=1, tiled=True)
    return (current[None], velocity_grad)


def solution(mesh):
    placed = (
        P("shot", None, "space"),
        P("shot", "space", None),
        P("shot", "space"),
        P("shot"),
        P("shot", "space", None, None),
        P("shot", "space", None, None),
        P("shot", None, "space", None, None),
        P("space", None, None),
    )
    return jax.shard_map(
        shards,
        mesh=mesh,
        in_specs=placed,
        out_specs=(P("shot", "space", None, None), P("space", "shot", None)),
        check_vma=False,
    )
```

profile of v0, /device:TPU:1, one launch (start us, length us, event | category | flops | bytes accessed | tf_op | source)
XLA Modules:
  0.0 969.0 jit_solution(18248099924798978966)
XLA Ops:
  7.9 132.5 %all-gather = s32[1,16384,1]{1,2,0:T(1,128)S(1)} all-gather(s32[1,256,1]{1,2,0:T(1,128)} %param.13), channel_id=2, replica_groups=mesh['shot'=4,'space'=64] {'space'}, dimensions={1}, use_global_device_ids=true | all-gather | bytes 66560 | tf_op jit(solution)/shard_map/all_gather | solution.py:74
  140.4 123.0 %all_gather.10 = s32[1,16384]{1,0:T(1,128)S(1)} all-gather(s32[1,256]{1,0:T(1,128)} %param.14), channel_id=1, replica_groups=mesh['shot'=4,'space'=64] {'space'}, dimensions={1}, use_global_device_ids=true | all-gather | bytes 66560 | tf_op jit(solution)/shard_map/all_gather | solution.py:75
  263.4 127.8 %all-gather.1 = f32[1,12,16384]{2,0,1:T(1,128)S(1)} all-gather(f32[1,12,256]{2,0,1:T(1,128)} %param.12), channel_id=3, replica_groups=mesh['shot'=4,'space'=64] {'space'}, dimensions={2}, use_global_device_ids=true | all-gather | bytes 798720 | tf_op jit(solution)/shard_map/all_gather | solution.py:73
  391.4 10.6 %fusion.36 = f32[12,512]{1,0:T(8,128)S(1)} fusion(s32[16384]{0:T(1024)S(1)} %fusion.40, f32[1,12,16384]{2,0,1:T(1,128)S(1)} %all-gather.1), kind=kOutput, calls=%fused_computation.58 | convolution fusion | flops 1216348160 | bytes 876544 | tf_op jit(solution)/shard_map/dot_general | solution.py:80
  405.3 7.0 copy.36
  412.3 383.4 %while.21 = (s32[]{:T(128)}, f32[8,64,256]{1,0,2:T(8,128)S(1)}, f32[8,64,256]{1,0,2:T(8,128)}, f32[8,64,256]{1,0,2:T(8,128)}, f32[8,64,256]{1,0,2:T(8,128)}, /*i...) while((s32[]{:T(128)}, f32[8,64,256]{1,0,2:T(8,128)S(1)}, ...), condition=%wide.region_1.2_spmd.clone, body=%wide.region_0.1_spmd.clone.sunk | while | flops 9936387 | bytes 35305808 | solution.py:94
  427.4 10.2 %fusion.47 = f32[8,64,256]{1,0,2:T(8,128)} fusion(f32[8,64,256]{1,0,2:T(8,128)} %get-tuple-element.335, f32[8,64,256]{1,0,2:T(8,128)S(1)} %get-tuple-element.323, f32[4,64,256]{1,0,2:T(4,128)} %collective-permute-done, f32[16,72,264]{1,0,2:T(8,128)S(1)} %select_maximum_fusion.3, f32[12,64,256]{1,0,2:T(8,128)} %copy-done, ...), kind=kLoop, calls=%fused_computation.25.clone.1 | loop fusion | flops 4849664 | bytes 12845056 | tf_op jit(solution)/shard_map/while/body/eval_jaxpr/add | solution.py:89
  458.9 10.2 %fusion.47 = f32[8,64,256]{1,0,2:T(8,128)} fusion(f32[8,64,256]{1,0,2:T(8,128)} %get-tuple-element.335, f32[8,64,256]{1,0,2:T(8,128)S(1)} %get-tuple-element.323, f32[4,64,256]{1,0,2:T(4,128)} %collective-permute-done, f32[16,72,264]{1,0,2:T(8,128)S(1)} %select_maximum_fusion.3, f32[12,64,256]{1,0,2:T(8,128)} %copy-done, ...), kind=kLoop, calls=%fused_computation.25.clone.1 | loop fusion | flops 4849664 | bytes 12845056 | tf_op jit(solution)/shard_map/while/body/eval_jaxpr/add | solution.py:89
  490.0 10.2 %fusion.47 = f32[8,64,256]{1,0,2:T(8,128)} fusion(f32[8,64,256]{1,0,2:T(8,128)} %get-tuple-element.335, f32[8,64,256]{1,0,2:T(8,128)S(1)} %get-tuple-element.323, f32[4,64,256]{1,0,2:T(4,128)} %collective-permute-done, f32[16,72,264]{1,0,2:T(8,128)S(1)} %select_maximum_fusion.3, f32[12,64,256]{1,0,2:T(8,128)} %copy-done, ...), kind=kLoop, calls=%fused_computation.25.clone.1 | loop fusion | flops 4849664 | bytes 12845056 | tf_op jit(solution)/shard_map/while/body/eval_jaxpr/add | solution.py:89
  521.0 10.2 %fusion.47 = f32[8,64,256]{1,0,2:T(8,128)} fusion(f32[8,64,256]{1,0,2:T(8,128)} %get-tuple-element.335, f32[8,64,256]{1,0,2:T(8,128)S(1)} %get-tuple-element.323, f32[4,64,256]{1,0,2:T(4,128)} %collective-permute-done, f32[16,72,264]{1,0,2:T(8,128)S(1)} %select_maximum_fusion.3, f32[12,64,256]{1,0,2:T(8,128)} %copy-done, ...), kind=kLoop, calls=%fused_computation.25.clone.1 | loop fusion | flops 4849664 | bytes 12845056 | tf_op jit(solution)/shard_map/while/body/eval_jaxpr/add | solution.py:89
  552.1 10.2 %fusion.47 = f32[8,64,256]{1,0,2:T(8,128)} fusion(f32[8,64,256]{1,0,2:T(8,128)} %get-tuple-element.335, f32[8,64,256]{1,0,2:T(8,128)S(1)} %get-tuple-element.323, f32[4,64,256]{1,0,2:T(4,128)} %collective-permute-done, f32[16,72,264]{1,0,2:T(8,128)S(1)} %select_maximum_fusion.3, f32[12,64,256]{1,0,2:T(8,128)} %copy-done, ...), kind=kLoop, calls=%fused_computation.25.clone.1 | loop fusion | flops 4849664 | bytes 12845056 | tf_op jit(solution)/shard_map/while/body/eval_jaxpr/add | solution.py:89
  583.1 10.2 %fusion.47 = f32[8,64,256]{1,0,2:T(8,128)} fusion(f32[8,64,256]{1,0,2:T(8,128)} %get-tuple-element.335, f32[8,64,256]{1,0,2:T(8,128)S(1)} %get-tuple-element.323, f32[4,64,256]{1,0,2:T(4,128)} %collective-permute-done, f32[16,72,264]{1,0,2:T(8,128)S(1)} %select_maximum_fusion.3, f32[12,64,256]{1,0,2:T(8,128)} %copy-done, ...), kind=kLoop, calls=%fused_computation.25.clone.1 | loop fusion | flops 4849664 | bytes 12845056 | tf_op jit(solution)/shard_map/while/body/eval_jaxpr/add | solution.py:89
  614.6 10.2 %fusion.47 = f32[8,64,256]{1,0,2:T(8,128)} fusion(f32[8,64,256]{1,0,2:T(8,128)} %get-tuple-element.335, f32[8,64,256]{1,0,2:T(8,128)S(1)} %get-tuple-element.323, f32[4,64,256]{1,0,2:T(4,128)} %collective-permute-done, f32[16,72,264]{1,0,2:T(8,128)S(1)} %select_maximum_fusion.3, f32[12,64,256]{1,0,2:T(8,128)} %copy-done, ...), kind=kLoop, calls=%fused_computation.25.clone.1 | loop fusion | flops 4849664 | bytes 12845056 | tf_op jit(solution)/shard_map/while/body/eval_jaxpr/add | solution.py:89
  632.5 6.0 collective-permute-start
  646.9 10.2 %fusion.47 = f32[8,64,256]{1,0,2:T(8,128)} fusion(f32[8,64,256]{1,0,2:T(8,128)} %get-tuple-element.335, f32[8,64,256]{1,0,2:T(8,128)S(1)} %get-tuple-element.323, f32[4,64,256]{1,0,2:T(4,128)} %collective-permute-done, f32[16,72,264]{1,0,2:T(8,128)S(1)} %select_maximum_fusion.3, f32[12,64,256]{1,0,2:T(8,128)} %copy-done, ...), kind=kLoop, calls=%fused_computation.25.clone.1 | loop fusion | flops 4849664 | bytes 12845056 | tf_op jit(solution)/shard_map/while/body/eval_jaxpr/add | solution.py:89
  664.8 6.0 collective-permute-start
  679.1 10.2 %fusion.47 = f32[8,64,256]{1,0,2:T(8,128)} fusion(f32[8,64,256]{1,0,2:T(8,128)} %get-tuple-element.335, f32[8,64,256]{1,0,2:T(8,128)S(1)} %get-tuple-element.323, f32[4,64,256]{1,0,2:T(4,128)} %collective-permute-done, f32[16,72,264]{1,0,2:T(8,128)S(1)} %select_maximum_fusion.3, f32[12,64,256]{1,0,2:T(8,128)} %copy-done, ...), kind=kLoop, calls=%fused_computation.25.clone.1 | loop fusion | flops 4849664 | bytes 12845056 | tf_op jit(solution)/shard_map/while/body/eval_jaxpr/add | solution.py:89
  697.1 6.0 collective-permute-start
  711.4 10.2 %fusion.47 = f32[8,64,256]{1,0,2:T(8,128)} fusion(f32[8,64,256]{1,0,2:T(8,128)} %get-tuple-element.335, f32[8,64,256]{1,0,2:T(8,128)S(1)} %get-tuple-element.323, f32[4,64,256]{1,0,2:T(4,128)} %collective-permute-done, f32[16,72,264]{1,0,2:T(8,128)S(1)} %select_maximum_fusion.3, f32[12,64,256]{1,0,2:T(8,128)} %copy-done, ...), kind=kLoop, calls=%fused_computation.25.clone.1 | loop fusion | flops 4849664 | bytes 12845056 | tf_op jit(solution)/shard_map/while/body/eval_jaxpr/add | solution.py:89
  729.3 6.0 collective-permute-start
  744.6 10.2 %fusion.47 = f32[8,64,256]{1,0,2:T(8,128)} fusion(f32[8,64,256]{1,0,2:T(8,128)} %get-tuple-element.335, f32[8,64,256]{1,0,2:T(8,128)S(1)} %get-tuple-element.323, f32[4,64,256]{1,0,2:T(4,128)} %collective-permute-done, f32[16,72,264]{1,0,2:T(8,128)S(1)} %select_maximum_fusion.3, f32[12,64,256]{1,0,2:T(8,128)} %copy-done, ...), kind=kLoop, calls=%fused_computation.25.clone.1 | loop fusion | flops 4849664 | bytes 12845056 | tf_op jit(solution)/shard_map/while/body/eval_jaxpr/add | solution.py:89
  762.5 6.5 collective-permute-start
  779.2 10.2 %fusion.47 = f32[8,64,256]{1,0,2:T(8,128)} fusion(f32[8,64,256]{1,0,2:T(8,128)} %get-tuple-element.335, f32[8,64,256]{1,0,2:T(8,128)S(1)} %get-tuple-element.323, f32[4,64,256]{1,0,2:T(4,128)} %collective-permute-done, f32[16,72,264]{1,0,2:T(8,128)S(1)} %select_maximum_fusion.3, f32[12,64,256]{1,0,2:T(8,128)} %copy-done, ...), kind=kLoop, calls=%fused_computation.25.clone.1 | loop fusion | flops 4849664 | bytes 12845056 | tf_op jit(solution)/shard_map/while/body/eval_jaxpr/add | solution.py:89
  799.2 162.9 %reduce-scatter.2.cloned.1.call-done = f32[8,16,256]{2,1,0:T(8,128)} async-done(((f32[8,64,256]{2,1,0:T(8,128)}), f32[8,16,256]{2,1,0:T(8,128)}) %reduce-scatter.2.cloned.1.call-update) | async-done | bytes 131088 | tf_op jit(solution)/shard_map/reduce_scatter | solution.py:97
  (276 shorter events, 237.1 us)
Async XLA Ops:
  7.2 955.0 %reduce-scatter.2.cloned.1.call-start = ((), (), s32[]{:S(2)}) async-start(), calls=%async_computation.1 | async-start | bytes 655360 | tf_op jit(solution)/shard_map/reduce_scatter | solution.py:97
  412.5 10.4 %collective-permute-start.1 = (f32[4,64,256]{1,0,2:T(4,128)S(1)}, f32[4,64,256]{1,0,2:T(4,128)S(1)}, u32[]{:S(2)}, u32[]{:S(2)}) collective-permute-start(f32[4,64,256]{1,0,2:T(4,128)S(1)} %get-tuple-element.312), channel_id=1, source_target_pairs={{1,0},{2,1},{3,2},{4,3},{5,4},{6,5},{7,6},{8,7},{9,8},{10,9},{11,1... | collective-permute-start | bytes 786440 | tf_op jit(solution)/shard_map/while/body/eval_jaxpr/ppermute | solution.py:17
  413.8 11.3 %collective-permute-start = (f32[4,64,256]{1,0,2:T(4,128)S(1)}, f32[4,64,256]{1,0,2:T(4,128)}, u32[]{:S(2)}, u32[]{:S(2)}) collective-permute-start(f32[4,64,256]{1,0,2:T(4,128)S(1)} %get-tuple-element.311), channel_id=1, source_target_pairs={{0,1},{1,2},{2,3},{3,4},{4,5},{5,6},{6,7},{7,8},{8,9},{9,10},{10,1... | collective-permute-start | bytes 786440 | tf_op jit(solution)/shard_map/while/body/eval_jaxpr/ppermute | solution.py:16
  444.1 10.4 %collective-permute-start.1 = (f32[4,64,256]{1,0,2:T(4,128)S(1)}, f32[4,64,256]{1,0,2:T(4,128)S(1)}, u32[]{:S(2)}, u32[]{:S(2)}) collective-permute-start(f32[4,64,256]{1,0,2:T(4,128)S(1)} %get-tuple-element.312), channel_id=1, source_target_pairs={{1,0},{2,1},{3,2},{4,3},{5,4},{6,5},{7,6},{8,7},{9,8},{10,9},{11,1... | collective-permute-start | bytes 786440 | tf_op jit(solution)/shard_map/while/body/eval_jaxpr/ppermute | solution.py:17
  445.4 11.2 %collective-permute-start = (f32[4,64,256]{1,0,2:T(4,128)S(1)}, f32[4,64,256]{1,0,2:T(4,128)}, u32[]{:S(2)}, u32[]{:S(2)}) collective-permute-start(f32[4,64,256]{1,0,2:T(4,128)S(1)} %get-tuple-element.311), channel_id=1, source_target_pairs={{0,1},{1,2},{2,3},{3,4},{4,5},{5,6},{6,7},{7,8},{8,9},{9,10},{10,1... | collective-permute-start | bytes 786440 | tf_op jit(solution)/shard_map/while/body/eval_jaxpr/ppermute | solution.py:16
  475.5 9.9 %collective-permute-start.1 = (f32[4,64,256]{1,0,2:T(4,128)S(1)}, f32[4,64,256]{1,0,2:T(4,128)S(1)}, u32[]{:S(2)}, u32[]{:S(2)}) collective-permute-start(f32[4,64,256]{1,0,2:T(4,128)S(1)} %get-tuple-element.312), channel_id=1, source_target_pairs={{1,0},{2,1},{3,2},{4,3},{5,4},{6,5},{7,6},{8,7},{9,8},{10,9},{11,1... | collective-permute-start | bytes 786440 | tf_op jit(solution)/shard_map/while/body/eval_jaxpr/ppermute | solution.py:17
  476.8 10.8 %collective-permute-start = (f32[4,64,256]{1,0,2:T(4,128)S(1)}, f32[4,64,256]{1,0,2:T(4,128)}, u32[]{:S(2)}, u32[]{:S(2)}) collective-permute-start(f32[4,64,256]{1,0,2:T(4,128)S(1)} %get-tuple-element.311), channel_id=1, source_target_pairs={{0,1},{1,2},{2,3},{3,4},{4,5},{5,6},{6,7},{7,8},{8,9},{9,10},{10,1... | collective-permute-start | bytes 786440 | tf_op jit(solution)/shard_map/while/body/eval_jaxpr/ppermute | solution.py:16
  506.6 9.9 %collective-permute-start.1 = (f32[4,64,256]{1,0,2:T(4,128)S(1)}, f32[4,64,256]{1,0,2:T(4,128)S(1)}, u32[]{:S(2)}, u32[]{:S(2)}) collective-permute-start(f32[4,64,256]{1,0,2:T(4,128)S(1)} %get-tuple-element.312), channel_id=1, source_target_pairs={{1,0},{2,1},{3,2},{4,3},{5,4},{6,5},{7,6},{8,7},{9,8},{10,9},{11,1... | collective-permute-start | bytes 786440 | tf_op jit(solution)/shard_map/while/body/eval_jaxpr/ppermute | solution.py:17
  507.9 10.8 %collective-permute-start = (f32[4,64,256]{1,0,2:T(4,128)S(1)}, f32[4,64,256]{1,0,2:T(4,128)}, u32[]{:S(2)}, u32[]{:S(2)}) collective-permute-start(f32[4,64,256]{1,0,2:T(4,128)S(1)} %get-tuple-element.311), channel_id=1, source_target_pairs={{0,1},{1,2},{2,3},{3,4},{4,5},{5,6},{6,7},{7,8},{8,9},{9,10},{10,1... | collective-permute-start | bytes 786440 | tf_op jit(solution)/shard_map/while/body/eval_jaxpr/ppermute | solution.py:16
  537.7 9.9 %collective-permute-start.1 = (f32[4,64,256]{1,0,2:T(4,128)S(1)}, f32[4,64,256]{1,0,2:T(4,128)S(1)}, u32[]{:S(2)}, u32[]{:S(2)}) collective-permute-start(f32[4,64,256]{1,0,2:T(4,128)S(1)} %get-tuple-element.312), channel_id=1, source_target_pairs={{1,0},{2,1},{3,2},{4,3},{5,4},{6,5},{7,6},{8,7},{9,8},{10,9},{11,1... | collective-permute-start | bytes 786440 | tf_op jit(solution)/shard_map/while/body/eval_jaxpr/ppermute | solution.py:17
  539.0 10.8 %collective-permute-start = (f32[4,64,256]{1,0,2:T(4,128)S(1)}, f32[4,64,256]{1,0,2:T(4,128)}, u32[]{:S(2)}, u32[]{:S(2)}) collective-permute-start(f32[4,64,256]{1,0,2:T(4,128)S(1)} %get-tuple-element.311), channel_id=1, source_target_pairs={{0,1},{1,2},{2,3},{3,4},{4,5},{5,6},{6,7},{7,8},{8,9},{9,10},{10,1... | collective-permute-start | bytes 786440 | tf_op jit(solution)/shard_map/while/body/eval_jaxpr/ppermute | solution.py:16
  570.0 10.8 %collective-permute-start = (f32[4,64,256]{1,0,2:T(4,128)S(1)}, f32[4,64,256]{1,0,2:T(4,128)}, u32[]{:S(2)}, u32[]{:S(2)}) collective-permute-start(f32[4,64,256]{1,0,2:T(4,128)S(1)} %get-tuple-element.311), channel_id=1, source_target_pairs={{0,1},{1,2},{2,3},{3,4},{4,5},{5,6},{6,7},{7,8},{8,9},{9,10},{10,1... | collective-permute-start | bytes 786440 | tf_op jit(solution)/shard_map/while/body/eval_jaxpr/ppermute | solution.py:16
  599.8 10.3 %collective-permute-start.1 = (f32[4,64,256]{1,0,2:T(4,128)S(1)}, f32[4,64,256]{1,0,2:T(4,128)S(1)}, u32[]{:S(2)}, u32[]{:S(2)}) collective-permute-start(f32[4,64,256]{1,0,2:T(4,128)S(1)} %get-tuple-element.312), channel_id=1, source_target_pairs={{1,0},{2,1},{3,2},{4,3},{5,4},{6,5},{7,6},{8,7},{9,8},{10,9},{11,1... | collective-permute-start | bytes 786440 | tf_op jit(solution)/shard_map/while/body/eval_jaxpr/ppermute | solution.py:17
  601.1 11.2 %collective-permute-start = (f32[4,64,256]{1,0,2:T(4,128)S(1)}, f32[4,64,256]{1,0,2:T(4,128)}, u32[]{:S(2)}, u32[]{:S(2)}) collective-permute-start(f32[4,64,256]{1,0,2:T(4,128)S(1)} %get-tuple-element.311), channel_id=1, source_target_pairs={{0,1},{1,2},{2,3},{3,4},{4,5},{5,6},{6,7},{7,8},{8,9},{9,10},{10,1... | collective-permute-start | bytes 786440 | tf_op jit(solution)/shard_map/while/body/eval_jaxpr/ppermute | solution.py:16
  631.2 11.1 %collective-permute-start.1 = (f32[4,64,256]{1,0,2:T(4,128)S(1)}, f32[4,64,256]{1,0,2:T(4,128)S(1)}, u32[]{:S(2)}, u32[]{:S(2)}) collective-permute-start(f32[4,64,256]{1,0,2:T(4,128)S(1)} %get-tuple-element.312), channel_id=1, source_target_pairs={{1,0},{2,1},{3,2},{4,3},{5,4},{6,5},{7,6},{8,7},{9,8},{10,9},{11,1... | collective-permute-start | bytes 786440 | tf_op jit(solution)/shard_map/while/body/eval_jaxpr/ppermute | solution.py:17
  632.5 12.0 %collective-permute-start = (f32[4,64,256]{1,0,2:T(4,128)S(1)}, f32[4,64,256]{1,0,2:T(4,128)}, u32[]{:S(2)}, u32[]{:S(2)}) collective-permute-start(f32[4,64,256]{1,0,2:T(4,128)S(1)} %get-tuple-element.311), channel_id=1, source_target_pairs={{0,1},{1,2},{2,3},{3,4},{4,5},{5,6},{6,7},{7,8},{8,9},{9,10},{10,1... | collective-permute-start | bytes 786440 | tf_op jit(solution)/shard_map/while/body/eval_jaxpr/ppermute | solution.py:16
  663.5 11.1 %collective-permute-start.1 = (f32[4,64,256]{1,0,2:T(4,128)S(1)}, f32[4,64,256]{1,0,2:T(4,128)S(1)}, u32[]{:S(2)}, u32[]{:S(2)}) collective-permute-start(f32[4,64,256]{1,0,2:T(4,128)S(1)} %get-tuple-element.312), channel_id=1, source_target_pairs={{1,0},{2,1},{3,2},{4,3},{5,4},{6,5},{7,6},{8,7},{9,8},{10,9},{11,1... | collective-permute-start | bytes 786440 | tf_op jit(solution)/shard_map/while/body/eval_jaxpr/ppermute | solution.py:17
  664.8 12.0 %collective-permute-start = (f32[4,64,256]{1,0,2:T(4,128)S(1)}, f32[4,64,256]{1,0,2:T(4,128)}, u32[]{:S(2)}, u32[]{:S(2)}) collective-permute-start(f32[4,64,256]{1,0,2:T(4,128)S(1)} %get-tuple-element.311), channel_id=1, source_target_pairs={{0,1},{1,2},{2,3},{3,4},{4,5},{5,6},{6,7},{7,8},{8,9},{9,10},{10,1... | collective-permute-start | bytes 786440 | tf_op jit(solution)/shard_map/while/body/eval_jaxpr/ppermute | solution.py:16
  695.8 11.1 %collective-permute-start.1 = (f32[4,64,256]{1,0,2:T(4,128)S(1)}, f32[4,64,256]{1,0,2:T(4,128)S(1)}, u32[]{:S(2)}, u32[]{:S(2)}) collective-permute-start(f32[4,64,256]{1,0,2:T(4,128)S(1)} %get-tuple-element.312), channel_id=1, source_target_pairs={{1,0},{2,1},{3,2},{4,3},{5,4},{6,5},{7,6},{8,7},{9,8},{10,9},{11,1... | collective-permute-start | bytes 786440 | tf_op jit(solution)/shard_map/while/body/eval_jaxpr/ppermute | solution.py:17
  697.1 12.0 %collective-permute-start = (f32[4,64,256]{1,0,2:T(4,128)S(1)}, f32[4,64,256]{1,0,2:T(4,128)}, u32[]{:S(2)}, u32[]{:S(2)}) collective-permute-start(f32[4,64,256]{1,0,2:T(4,128)S(1)} %get-tuple-element.311), channel_id=1, source_target_pairs={{0,1},{1,2},{2,3},{3,4},{4,5},{5,6},{6,7},{7,8},{8,9},{9,10},{10,1... | collective-permute-start | bytes 786440 | tf_op jit(solution)/shard_map/while/body/eval_jaxpr/ppermute | solution.py:16
  728.0 12.0 %collective-permute-start.1 = (f32[4,64,256]{1,0,2:T(4,128)S(1)}, f32[4,64,256]{1,0,2:T(4,128)S(1)}, u32[]{:S(2)}, u32[]{:S(2)}) collective-permute-start(f32[4,64,256]{1,0,2:T(4,128)S(1)} %get-tuple-element.312), channel_id=1, source_target_pairs={{1,0},{2,1},{3,2},{4,3},{5,4},{6,5},{7,6},{8,7},{9,8},{10,9},{11,1... | collective-permute-start | bytes 786440 | tf_op jit(solution)/shard_map/while/body/eval_jaxpr/ppermute | solution.py:17
  729.3 12.9 %collective-permute-start = (f32[4,64,256]{1,0,2:T(4,128)S(1)}, f32[4,64,256]{1,0,2:T(4,128)}, u32[]{:S(2)}, u32[]{:S(2)}) collective-permute-start(f32[4,64,256]{1,0,2:T(4,128)S(1)} %get-tuple-element.311), channel_id=1, source_target_pairs={{0,1},{1,2},{2,3},{3,4},{4,5},{5,6},{6,7},{7,8},{8,9},{9,10},{10,1... | collective-permute-start | bytes 786440 | tf_op jit(solution)/shard_map/while/body/eval_jaxpr/ppermute | solution.py:16
  761.2 13.5 %collective-permute-start.1 = (f32[4,64,256]{1,0,2:T(4,128)S(1)}, f32[4,64,256]{1,0,2:T(4,128)S(1)}, u32[]{:S(2)}, u32[]{:S(2)}) collective-permute-start(f32[4,64,256]{1,0,2:T(4,128)S(1)} %get-tuple-element.312), channel_id=1, source_target_pairs={{1,0},{2,1},{3,2},{4,3},{5,4},{6,5},{7,6},{8,7},{9,8},{10,9},{11,1... | collective-permute-start | bytes 786440 | tf_op jit(solution)/shard_map/while/body/eval_jaxpr/ppermute | solution.py:17
  762.5 14.4 %collective-permute-start = (f32[4,64,256]{1,0,2:T(4,128)S(1)}, f32[4,64,256]{1,0,2:T(4,128)}, u32[]{:S(2)}, u32[]{:S(2)}) collective-permute-start(f32[4,64,256]{1,0,2:T(4,128)S(1)} %get-tuple-element.311), channel_id=1, source_target_pairs={{0,1},{1,2},{2,3},{3,4},{4,5},{5,6},{6,7},{7,8},{8,9},{9,10},{10,1... | collective-permute-start | bytes 786440 | tf_op jit(solution)/shard_map/while/body/eval_jaxpr/ppermute | solution.py:16
  (64 other events, 132.7 us)
Sparse Core Ops, SparseCore 0:
  798.2 163.8 reduce-scatter.1
where the time goes:
time: 971 us; the launch traced here: 969 us
  blocking collectives  383 us (39%)
  waiting for transfers between devices  211 us (22%)
  other arithmetic  184 us (19%)
  local copies, waits for them, and re-layouts  84.5 us (9%)
  starting transfers between devices  80.2 us (8%)
  between operations  14.7 us (2%)
  matrix products  10.6 us (1%)
    reduce_scatter x1, waiting for transfers between devices, shards(): lax.psum_scatter(gradient, 'shot', scatter_dimension=1, tiled=True)  163 us
    all_gather x1, blocking collectives, shards(): lax.all_gather(owner_row[None, :], 'space', axis=1, tiled=True)  133 us
    all_gather x1, blocking collectives, shards(): piece_traces = lax.all_gather(traces, 'space', axis=1, tiled=True)  128 us
    all_gather x1, blocking collectives, shards(): lax.all_gather(surface[None, :], 'space', axis=1, tiled=True)  123 us
    add x12, other arithmetic, advance(): fresh = 2.0 * current - later + courant_sq * laplace_rim(extended)  122 us
    while x156, local copies, waits for them, and re-layouts  67.3 us
    ppermute x12, starting transfers between devices, extended_2(): before = lax.ppermute(last, axis, up)  64.7 us
    ppermute x12, waiting for transfers between devices, extended_2(): after = lax.ppermute(leading, axis, down)  48.5 us
  transfers between devices with their start and end apart: 25, of which 13 were waited for; matrix products, arithmetic and copies ran while one was open for 0% of the time, Pallas kernels for 0%

commit v1 on v0

--- a/solution.py
+++ b/solution.py
@@ -72,7 +72,10 @@
     my_index = lax.axis_index("space")
     piece_traces = lax.all_gather(traces, "space", axis=1, tiled=True)
     piece_owner = lax.all_gather(owner_row[None, :], "space", axis=1, tiled=True)
-    piece_surface = lax.all_gather(surface[None, :], "space", axis=1, tiled=True)
+    piece_surface = jnp.concatenate(
+        lax.all_to_all(jnp.stack([surface[None, :]] * lax.axis_size("space")), "space", 0, 0),
+        axis=1,
+    )
     number = jnp.arange(piece_traces.shape[1], dtype=jnp.int32)
     keep = (number < live_count) & (piece_owner[0] == my_index)
     targets = jnp.where(keep, piece_surface[0], -1)

time: 971 us -> 837 us (0.86)
  blocking collectives: 383 us -> 255 us
  waiting for transfers between devices: 211 us -> 186 us
  starting transfers between devices: 80.2 us -> 95.5 us
    all_gather x1 -> x0, blocking collectives: 123 us -> none  [shards(): lax.all_gather(surface[None, :], 'space', axis=1, tiled=True)]
    reduce_scatter x1, waiting for transfers between devices: 163 us -> 108 us  [shards(): lax.psum_scatter(gradient, 'shot', scatter_dimension=1, tiled=True)]
    ppermute x12, waiting for transfers between devices: 48.5 us -> 77.9 us  [extended_2(): after = lax.ppermute(leading, axis, down)]
    all_to_all x0 -> x1, starting transfers between devices: none -> 13.6 us  [shards(): lax.all_to_all(jnp.stack([surface[None, :]] * lax.axis_size('space')), 's...]
    all_gather x1, blocking collectives: 133 us -> 123 us  [shards(): lax.all_gather(owner_row[None, :], 'space', axis=1, tiled=True)]
  transfers between devices with their start and end apart: 25 -> 26, of which waited for: 13 -> 13; matrix products, arithmetic and copies ran while one was open for 0% -> 2% of each run, Pallas kernels for 0% -> 0%
where the time goes in v1:
time: 837 us; the launch traced here: 834 us
  blocking collectives  255 us (30%)
  waiting for transfers between devices  186 us (22%)
  other arithmetic  185 us (22%)
  starting transfers between devices  95.5 us (11%)
  local copies, waits for them, and re-layouts  86.4 us (10%)
  between operations  14.7 us (2%)
  matrix products  10.6 us (1%)
    all_gather x1, blocking collectives, shards(): piece_traces = lax.all_gather(traces, 'space', axis=1, tiled=True)  133 us
    add x12, other arithmetic, advance(): fresh = 2.0 * current - later + courant_sq * laplace_rim(extended)  123 us
    all_gather x1, blocking collectives, shards(): lax.all_gather(owner_row[None, :], 'space', axis=1, tiled=True)  123 us
    reduce_scatter x1, waiting for transfers between devices, shards(): lax.psum_scatter(gradient, 'shot', scatter_dimension=1, tiled=True)  108 us
    ppermute x12, waiting for transfers between devices, extended_2(): after = lax.ppermute(leading, axis, down)  77.9 us
    while x156, local copies, waits for them, and re-layouts  66.7 us
    ppermute x12, starting transfers between devices, extended_2(): before = lax.ppermute(last, axis, up)  66.3 us
    concatenate x12, other arithmetic, extended_2(): shard = jnp.concatenate([before, shard, after], axis=dim)  28.2 us
  transfers between devices with their start and end apart: 26, of which 13 were waited for; matrix products, arithmetic and copies ran while one was open for 2% of the time, Pallas kernels for 0%

profile of v1, /device:TPU:1, one launch (start us, length us, event | category | flops | bytes accessed | tf_op | source)
XLA Modules:
  0.0 834.2 jit_solution(7289668024525152601)
XLA Ops:
  8.6 13.6 %all-to-all-start = ((s32[64,1,256]{2,1,0:T(1,128)}), s32[64,1,256]{2,1,0:T(1,128)S(1)}, u32[]{:S(2)}, u32[]{:S(2)}) async-start(s32[64,1,256]{2,1,0:T(1,128)} %stack.3), calls=%async_computation | async-start | bytes 131072 | tf_op jit(solution)/shard_map/all_to_all | solution.py:76
  22.3 132.8 %all-gather.1 = f32[1,12,16384]{2,0,1:T(1,128)S(1)} all-gather(f32[1,12,256]{2,0,1:T(1,128)} %param.12), channel_id=3, replica_groups=mesh['shot'=4,'space'=64] {'space'}, dimensions={2}, use_global_device_ids=true | all-gather | bytes 798720 | tf_op jit(solution)/shard_map/all_gather | solution.py:73
  155.0 122.6 %all-gather = s32[1,16384,1]{1,2,0:T(1,128)S(1)} all-gather(s32[1,256,1]{1,2,0:T(1,128)} %param.13), channel_id=2, replica_groups=mesh['shot'=4,'space'=64] {'space'}, dimensions={1}, use_global_device_ids=true | all-gather | bytes 66560 | tf_op jit(solution)/shard_map/all_gather | solution.py:74
  289.8 10.6 %fusion.36 = f32[12,512]{1,0:T(8,128)S(1)} fusion(s32[16384]{0:T(1024)S(1)} %fusion.40, f32[1,12,16384]{2,0,1:T(1,128)S(1)} %all-gather.1), kind=kOutput, calls=%fused_computation.58 | convolution fusion | flops 1216348160 | bytes 876544 | tf_op jit(solution)/shard_map/dot_general | solution.py:83
  300.4 415.0 %while.21 = (s32[]{:T(128)}, f32[8,64,256]{1,0,2:T(8,128)S(1)}, f32[8,64,256]{1,0,2:T(8,128)}, f32[8,64,256]{1,0,2:T(8,128)}, f32[8,64,256]{1,0,2:T(8,128)}, /*i...) while((s32[]{:T(128)}, f32[8,64,256]{1,0,2:T(8,128)S(1)}, ...), condition=%wide.region_1.2_spmd.clone, body=%wide.region_0.1_spmd.clone.sunk | while | flops 9936387 | bytes 35305808 | solution.py:97
  315.4 10.2 %fusion.47 = f32[8,64,256]{1,0,2:T(8,128)} fusion(f32[8,64,256]{1,0,2:T(8,128)} %get-tuple-element.335, f32[8,64,256]{1,0,2:T(8,128)S(1)} %get-tuple-element.323, f32[4,64,256]{1,0,2:T(4,128)} %collective-permute-done, f32[16,72,264]{1,0,2:T(8,128)S(1)} %select_maximum_fusion.3, f32[12,64,256]{1,0,2:T(8,128)} %copy-done, ...), kind=kLoop, calls=%fused_computation.25.clone.1 | loop fusion | flops 4849664 | bytes 12845056 | tf_op jit(solution)/shard_map/while/body/eval_jaxpr/add | solution.py:92
  346.6 10.2 %fusion.47 = f32[8,64,256]{1,0,2:T(8,128)} fusion(f32[8,64,256]{1,0,2:T(8,128)} %get-tuple-element.335, f32[8,64,256]{1,0,2:T(8,128)S(1)} %get-tuple-element.323, f32[4,64,256]{1,0,2:T(4,128)} %collective-permute-done, f32[16,72,264]{1,0,2:T(8,128)S(1)} %select_maximum_fusion.3, f32[12,64,256]{1,0,2:T(8,128)} %copy-done, ...), kind=kLoop, calls=%fused_computation.25.clone.1 | loop fusion | flops 4849664 | bytes 12845056 | tf_op jit(solution)/shard_map/while/body/eval_jaxpr/add | solution.py:92
  377.7 10.2 %fusion.47 = f32[8,64,256]{1,0,2:T(8,128)} fusion(f32[8,64,256]{1,0,2:T(8,128)} %get-tuple-element.335, f32[8,64,256]{1,0,2:T(8,128)S(1)} %get-tuple-element.323, f32[4,64,256]{1,0,2:T(4,128)} %collective-permute-done, f32[16,72,264]{1,0,2:T(8,128)S(1)} %select_maximum_fusion.3, f32[12,64,256]{1,0,2:T(8,128)} %copy-done, ...), kind=kLoop, calls=%fused_computation.25.clone.1 | loop fusion | flops 4849664 | bytes 12845056 | tf_op jit(solution)/shard_map/while/body/eval_jaxpr/add | solution.py:92
  410.0 10.2 %fusion.47 = f32[8,64,256]{1,0,2:T(8,128)} fusion(f32[8,64,256]{1,0,2:T(8,128)} %get-tuple-element.335, f32[8,64,256]{1,0,2:T(8,128)S(1)} %get-tuple-element.323, f32[4,64,256]{1,0,2:T(4,128)} %collective-permute-done, f32[16,72,264]{1,0,2:T(8,128)S(1)} %select_maximum_fusion.3, f32[12,64,256]{1,0,2:T(8,128)} %copy-done, ...), kind=kLoop, calls=%fused_computation.25.clone.1 | loop fusion | flops 4849664 | bytes 12845056 | tf_op jit(solution)/shard_map/while/body/eval_jaxpr/add | solution.py:92
  443.4 10.2 %fusion.47 = f32[8,64,256]{1,0,2:T(8,128)} fusion(f32[8,64,256]{1,0,2:T(8,128)} %get-tuple-element.335, f32[8,64,256]{1,0,2:T(8,128)S(1)} %get-tuple-element.323, f32[4,64,256]{1,0,2:T(4,128)} %collective-permute-done, f32[16,72,264]{1,0,2:T(8,128)S(1)} %select_maximum_fusion.3, f32[12,64,256]{1,0,2:T(8,128)} %copy-done, ...), kind=kLoop, calls=%fused_computation.25.clone.1 | loop fusion | flops 4849664 | bytes 12845056 | tf_op jit(solution)/shard_map/while/body/eval_jaxpr/add | solution.py:92
  478.0 10.2 %fusion.47 = f32[8,64,256]{1,0,2:T(8,128)} fusion(f32[8,64,256]{1,0,2:T(8,128)} %get-tuple-element.335, f32[8,64,256]{1,0,2:T(8,128)S(1)} %get-tuple-element.323, f32[4,64,256]{1,0,2:T(4,128)} %collective-permute-done, f32[16,72,264]{1,0,2:T(8,128)S(1)} %select_maximum_fusion.3, f32[12,64,256]{1,0,2:T(8,128)} %copy-done, ...), kind=kLoop, calls=%fused_computation.25.clone.1 | loop fusion | flops 4849664 | bytes 12845056 | tf_op jit(solution)/shard_map/while/body/eval_jaxpr/add | solution.py:92
  501.3 7.7 collective-permute-done.1
  513.5 10.2 %fusion.47 = f32[8,64,256]{1,0,2:T(8,128)} fusion(f32[8,64,256]{1,0,2:T(8,128)} %get-tuple-element.335, f32[8,64,256]{1,0,2:T(8,128)S(1)} %get-tuple-element.323, f32[4,64,256]{1,0,2:T(4,128)} %collective-permute-done, f32[16,72,264]{1,0,2:T(8,128)S(1)} %select_maximum_fusion.3, f32[12,64,256]{1,0,2:T(8,128)} %copy-done, ...), kind=kLoop, calls=%fused_computation.25.clone.1 | loop fusion | flops 4849664 | bytes 12845056 | tf_op jit(solution)/shard_map/while/body/eval_jaxpr/add | solution.py:92
  537.6 8.0 collective-permute-done.1
  550.1 10.2 %fusion.47 = f32[8,64,256]{1,0,2:T(8,128)} fusion(f32[8,64,256]{1,0,2:T(8,128)} %get-tuple-element.335, f32[8,64,256]{1,0,2:T(8,128)S(1)} %get-tuple-element.323, f32[4,64,256]{1,0,2:T(4,128)} %collective-permute-done, f32[16,72,264]{1,0,2:T(8,128)S(1)} %select_maximum_fusion.3, f32[12,64,256]{1,0,2:T(8,128)} %copy-done, ...), kind=kLoop, calls=%fused_computation.25.clone.1 | loop fusion | flops 4849664 | bytes 12845056 | tf_op jit(solution)/shard_map/while/body/eval_jaxpr/add | solution.py:92
  575.2 9.5 %collective-permute-done.1 = f32[4,64,256]{1,0,2:T(4,128)S(1)} collective-permute-done((f32[4,64,256]{1,0,2:T(4,128)S(1)}, f32[4,64,256]{1,0,2:T(4,128)S(1)}, u32[]{:S(2)}, u32[]{:S(2)}) %collective-permute-start.1) | collective-permute-done | bytes 262176 | tf_op jit(solution)/shard_map/while/body/eval_jaxpr/ppermute | solution.py:17
  589.1 10.2 %fusion.47 = f32[8,64,256]{1,0,2:T(8,128)} fusion(f32[8,64,256]{1,0,2:T(8,128)} %get-tuple-element.335, f32[8,64,256]{1,0,2:T(8,128)S(1)} %get-tuple-element.323, f32[4,64,256]{1,0,2:T(4,128)} %collective-permute-done, f32[16,72,264]{1,0,2:T(8,128)S(1)} %select_maximum_fusion.3, f32[12,64,256]{1,0,2:T(8,128)} %copy-done, ...), kind=kLoop, calls=%fused_computation.25.clone.1 | loop fusion | flops 4849664 | bytes 12845056 | tf_op jit(solution)/shard_map/while/body/eval_jaxpr/add | solution.py:92
  614.2 8.9 %collective-permute-done.1 = f32[4,64,256]{1,0,2:T(4,128)S(1)} collective-permute-done((f32[4,64,256]{1,0,2:T(4,128)S(1)}, f32[4,64,256]{1,0,2:T(4,128)S(1)}, u32[]{:S(2)}, u32[]{:S(2)}) %collective-permute-start.1) | collective-permute-done | bytes 262176 | tf_op jit(solution)/shard_map/while/body/eval_jaxpr/ppermute | solution.py:17
  627.6 10.2 %fusion.47 = f32[8,64,256]{1,0,2:T(8,128)} fusion(f32[8,64,256]{1,0,2:T(8,128)} %get-tuple-element.335, f32[8,64,256]{1,0,2:T(8,128)S(1)} %get-tuple-element.323, f32[4,64,256]{1,0,2:T(4,128)} %collective-permute-done, f32[16,72,264]{1,0,2:T(8,128)S(1)} %select_maximum_fusion.3, f32[12,64,256]{1,0,2:T(8,128)} %copy-done, ...), kind=kLoop, calls=%fused_computation.25.clone.1 | loop fusion | flops 4849664 | bytes 12845056 | tf_op jit(solution)/shard_map/while/body/eval_jaxpr/add | solution.py:92
  651.8 8.1 collective-permute-done.1
  664.4 10.2 %fusion.47 = f32[8,64,256]{1,0,2:T(8,128)} fusion(f32[8,64,256]{1,0,2:T(8,128)} %get-tuple-element.335, f32[8,64,256]{1,0,2:T(8,128)S(1)} %get-tuple-element.323, f32[4,64,256]{1,0,2:T(4,128)} %collective-permute-done, f32[16,72,264]{1,0,2:T(8,128)S(1)} %select_maximum_fusion.3, f32[12,64,256]{1,0,2:T(8,128)} %copy-done, ...), kind=kLoop, calls=%fused_computation.25.clone.1 | loop fusion | flops 4849664 | bytes 12845056 | tf_op jit(solution)/shard_map/while/body/eval_jaxpr/add | solution.py:92
  687.3 7.2 collective-permute-done.1
  698.9 10.2 %fusion.47 = f32[8,64,256]{1,0,2:T(8,128)} fusion(f32[8,64,256]{1,0,2:T(8,128)} %get-tuple-element.335, f32[8,64,256]{1,0,2:T(8,128)S(1)} %get-tuple-element.323, f32[4,64,256]{1,0,2:T(4,128)} %collective-permute-done, f32[16,72,264]{1,0,2:T(8,128)S(1)} %select_maximum_fusion.3, f32[12,64,256]{1,0,2:T(8,128)} %copy-done, ...), kind=kLoop, calls=%fused_computation.25.clone.1 | loop fusion | flops 4849664 | bytes 12845056 | tf_op jit(solution)/shard_map/while/body/eval_jaxpr/add | solution.py:92
  719.0 108.4 %reduce-scatter.2.cloned.1.call-done = f32[8,16,256]{2,1,0:T(8,128)} async-done(((f32[8,64,256]{2,1,0:T(8,128)}), f32[8,16,256]{2,1,0:T(8,128)}) %reduce-scatter.2.cloned.1.call-update) | async-done | bytes 131088 | tf_op jit(solution)/shard_map/reduce_scatter | solution.py:100
  (276 shorter events, 258.6 us)
Async XLA Ops:
  8.6 281.1 %all-to-all-start = ((s32[64,1,256]{2,1,0:T(1,128)}), s32[64,1,256]{2,1,0:T(1,128)S(1)}, u32[]{:S(2)}, u32[]{:S(2)}) async-start(s32[64,1,256]{2,1,0:T(1,128)} %stack.3), calls=%async_computation | async-start | bytes 131072 | tf_op jit(solution)/shard_map/all_to_all | solution.py:76
  22.2 805.2 %reduce-scatter.2.cloned.1.call-start = ((), (), s32[]{:S(2)}) async-start(), calls=%async_computation.2 | async-start | bytes 655360 | tf_op jit(solution)/shard_map/reduce_scatter | solution.py:100
  300.8 10.1 %collective-permute-start.1 = (f32[4,64,256]{1,0,2:T(4,128)S(1)}, f32[4,64,256]{1,0,2:T(4,128)S(1)}, u32[]{:S(2)}, u32[]{:S(2)}) collective-permute-start(f32[4,64,256]{1,0,2:T(4,128)S(1)} %get-tuple-element.312), channel_id=1, source_target_pairs={{1,0},{2,1},{3,2},{4,3},{5,4},{6,5},{7,6},{8,7},{9,8},{10,9},{11,1... | collective-permute-start | bytes 786440 | tf_op jit(solution)/shard_map/while/body/eval_jaxpr/ppermute | solution.py:17
  302.1 11.0 %collective-permute-start = (f32[4,64,256]{1,0,2:T(4,128)S(1)}, f32[4,64,256]{1,0,2:T(4,128)}, u32[]{:S(2)}, u32[]{:S(2)}) collective-permute-start(f32[4,64,256]{1,0,2:T(4,128)S(1)} %get-tuple-element.311), channel_id=1, source_target_pairs={{0,1},{1,2},{2,3},{3,4},{4,5},{5,6},{6,7},{7,8},{8,9},{9,10},{10,1... | collective-permute-start | bytes 786440 | tf_op jit(solution)/shard_map/while/body/eval_jaxpr/ppermute | solution.py:16
  333.4 10.9 %collective-permute-start = (f32[4,64,256]{1,0,2:T(4,128)S(1)}, f32[4,64,256]{1,0,2:T(4,128)}, u32[]{:S(2)}, u32[]{:S(2)}) collective-permute-start(f32[4,64,256]{1,0,2:T(4,128)S(1)} %get-tuple-element.311), channel_id=1, source_target_pairs={{0,1},{1,2},{2,3},{3,4},{4,5},{5,6},{6,7},{7,8},{8,9},{9,10},{10,1... | collective-permute-start | bytes 786440 | tf_op jit(solution)/shard_map/while/body/eval_jaxpr/ppermute | solution.py:16
  364.6 10.8 %collective-permute-start = (f32[4,64,256]{1,0,2:T(4,128)S(1)}, f32[4,64,256]{1,0,2:T(4,128)}, u32[]{:S(2)}, u32[]{:S(2)}) collective-permute-start(f32[4,64,256]{1,0,2:T(4,128)S(1)} %get-tuple-element.311), channel_id=1, source_target_pairs={{0,1},{1,2},{2,3},{3,4},{4,5},{5,6},{6,7},{7,8},{8,9},{9,10},{10,1... | collective-permute-start | bytes 786440 | tf_op jit(solution)/shard_map/while/body/eval_jaxpr/ppermute | solution.py:16
  394.3 11.1 %collective-permute-start.1 = (f32[4,64,256]{1,0,2:T(4,128)S(1)}, f32[4,64,256]{1,0,2:T(4,128)S(1)}, u32[]{:S(2)}, u32[]{:S(2)}) collective-permute-start(f32[4,64,256]{1,0,2:T(4,128)S(1)} %get-tuple-element.312), channel_id=1, source_target_pairs={{1,0},{2,1},{3,2},{4,3},{5,4},{6,5},{7,6},{8,7},{9,8},{10,9},{11,1... | collective-permute-start | bytes 786440 | tf_op jit(solution)/shard_map/while/body/eval_jaxpr/ppermute | solution.py:17
  395.6 12.0 %collective-permute-start = (f32[4,64,256]{1,0,2:T(4,128)S(1)}, f32[4,64,256]{1,0,2:T(4,128)}, u32[]{:S(2)}, u32[]{:S(2)}) collective-permute-start(f32[4,64,256]{1,0,2:T(4,128)S(1)} %get-tuple-element.311), channel_id=1, source_target_pairs={{0,1},{1,2},{2,3},{3,4},{4,5},{5,6},{6,7},{7,8},{8,9},{9,10},{10,1... | collective-permute-start | bytes 786440 | tf_op jit(solution)/shard_map/while/body/eval_jaxpr/ppermute | solution.py:16
  426.6 12.3 %collective-permute-start.1 = (f32[4,64,256]{1,0,2:T(4,128)S(1)}, f32[4,64,256]{1,0,2:T(4,128)S(1)}, u32[]{:S(2)}, u32[]{:S(2)}) collective-permute-start(f32[4,64,256]{1,0,2:T(4,128)S(1)} %get-tuple-element.312), channel_id=1, source_target_pairs={{1,0},{2,1},{3,2},{4,3},{5,4},{6,5},{7,6},{8,7},{9,8},{10,9},{11,1... | collective-permute-start | bytes 786440 | tf_op jit(solution)/shard_map/while/body/eval_jaxpr/ppermute | solution.py:17
  427.9 13.2 %collective-permute-start = (f32[4,64,256]{1,0,2:T(4,128)S(1)}, f32[4,64,256]{1,0,2:T(4,128)}, u32[]{:S(2)}, u32[]{:S(2)}) collective-permute-start(f32[4,64,256]{1,0,2:T(4,128)S(1)} %get-tuple-element.311), channel_id=1, source_target_pairs={{0,1},{1,2},{2,3},{3,4},{4,5},{5,6},{6,7},{7,8},{8,9},{9,10},{10,1... | collective-permute-start | bytes 786440 | tf_op jit(solution)/shard_map/while/body/eval_jaxpr/ppermute | solution.py:16
  460.1 13.4 %collective-permute-start.1 = (f32[4,64,256]{1,0,2:T(4,128)S(1)}, f32[4,64,256]{1,0,2:T(4,128)S(1)}, u32[]{:S(2)}, u32[]{:S(2)}) collective-permute-start(f32[4,64,256]{1,0,2:T(4,128)S(1)} %get-tuple-element.312), channel_id=1, source_target_pairs={{1,0},{2,1},{3,2},{4,3},{5,4},{6,5},{7,6},{8,7},{9,8},{10,9},{11,1... | collective-permute-start | bytes 786440 | tf_op jit(solution)/shard_map/while/body/eval_jaxpr/ppermute | solution.py:17
  461.4 14.2 %collective-permute-start = (f32[4,64,256]{1,0,2:T(4,128)S(1)}, f32[4,64,256]{1,0,2:T(4,128)}, u32[]{:S(2)}, u32[]{:S(2)}) collective-permute-start(f32[4,64,256]{1,0,2:T(4,128)S(1)} %get-tuple-element.311), channel_id=1, source_target_pairs={{0,1},{1,2},{2,3},{3,4},{4,5},{5,6},{6,7},{7,8},{8,9},{9,10},{10,1... | collective-permute-start | bytes 786440 | tf_op jit(solution)/shard_map/while/body/eval_jaxpr/ppermute | solution.py:16
  494.7 14.4 %collective-permute-start.1 = (f32[4,64,256]{1,0,2:T(4,128)S(1)}, f32[4,64,256]{1,0,2:T(4,128)S(1)}, u32[]{:S(2)}, u32[]{:S(2)}) collective-permute-start(f32[4,64,256]{1,0,2:T(4,128)S(1)} %get-tuple-element.312), channel_id=1, source_target_pairs={{1,0},{2,1},{3,2},{4,3},{5,4},{6,5},{7,6},{8,7},{9,8},{10,9},{11,1... | collective-permute-start | bytes 786440 | tf_op jit(solution)/shard_map/while/body/eval_jaxpr/ppermute | solution.py:17
  496.0 15.2 %collective-permute-start = (f32[4,64,256]{1,0,2:T(4,128)S(1)}, f32[4,64,256]{1,0,2:T(4,128)}, u32[]{:S(2)}, u32[]{:S(2)}) collective-permute-start(f32[4,64,256]{1,0,2:T(4,128)S(1)} %get-tuple-element.311), channel_id=1, source_target_pairs={{0,1},{1,2},{2,3},{3,4},{4,5},{5,6},{6,7},{7,8},{8,9},{9,10},{10,1... | collective-permute-start | bytes 786440 | tf_op jit(solution)/shard_map/while/body/eval_jaxpr/ppermute | solution.py:16
  530.2 15.4 %collective-permute-start.1 = (f32[4,64,256]{1,0,2:T(4,128)S(1)}, f32[4,64,256]{1,0,2:T(4,128)S(1)}, u32[]{:S(2)}, u32[]{:S(2)}) collective-permute-start(f32[4,64,256]{1,0,2:T(4,128)S(1)} %get-tuple-element.312), channel_id=1, source_target_pairs={{1,0},{2,1},{3,2},{4,3},{5,4},{6,5},{7,6},{8,7},{9,8},{10,9},{11,1... | collective-permute-start | bytes 786440 | tf_op jit(solution)/shard_map/while/body/eval_jaxpr/ppermute | solution.py:17
  531.5 16.3 %collective-permute-start = (f32[4,64,256]{1,0,2:T(4,128)S(1)}, f32[4,64,256]{1,0,2:T(4,128)}, u32[]{:S(2)}, u32[]{:S(2)}) collective-permute-start(f32[4,64,256]{1,0,2:T(4,128)S(1)} %get-tuple-element.311), channel_id=1, source_target_pairs={{0,1},{1,2},{2,3},{3,4},{4,5},{5,6},{6,7},{7,8},{8,9},{9,10},{10,1... | collective-permute-start | bytes 786440 | tf_op jit(solution)/shard_map/while/body/eval_jaxpr/ppermute | solution.py:16
  566.8 17.9 %collective-permute-start.1 = (f32[4,64,256]{1,0,2:T(4,128)S(1)}, f32[4,64,256]{1,0,2:T(4,128)S(1)}, u32[]{:S(2)}, u32[]{:S(2)}) collective-permute-start(f32[4,64,256]{1,0,2:T(4,128)S(1)} %get-tuple-element.312), channel_id=1, source_target_pairs={{1,0},{2,1},{3,2},{4,3},{5,4},{6,5},{7,6},{8,7},{9,8},{10,9},{11,1... | collective-permute-start | bytes 786440 | tf_op jit(solution)/shard_map/while/body/eval_jaxpr/ppermute | solution.py:17
  568.1 18.7 %collective-permute-start = (f32[4,64,256]{1,0,2:T(4,128)S(1)}, f32[4,64,256]{1,0,2:T(4,128)}, u32[]{:S(2)}, u32[]{:S(2)}) collective-permute-start(f32[4,64,256]{1,0,2:T(4,128)S(1)} %get-tuple-element.311), channel_id=1, source_target_pairs={{0,1},{1,2},{2,3},{3,4},{4,5},{5,6},{6,7},{7,8},{8,9},{9,10},{10,1... | collective-permute-start | bytes 786440 | tf_op jit(solution)/shard_map/while/body/eval_jaxpr/ppermute | solution.py:16
  605.8 17.3 %collective-permute-start.1 = (f32[4,64,256]{1,0,2:T(4,128)S(1)}, f32[4,64,256]{1,0,2:T(4,128)S(1)}, u32[]{:S(2)}, u32[]{:S(2)}) collective-permute-start(f32[4,64,256]{1,0,2:T(4,128)S(1)} %get-tuple-element.312), channel_id=1, source_target_pairs={{1,0},{2,1},{3,2},{4,3},{5,4},{6,5},{7,6},{8,7},{9,8},{10,9},{11,1... | collective-permute-start | bytes 786440 | tf_op jit(solution)/shard_map/while/body/eval_jaxpr/ppermute | solution.py:17
  607.1 18.1 %collective-permute-start = (f32[4,64,256]{1,0,2:T(4,128)S(1)}, f32[4,64,256]{1,0,2:T(4,128)}, u32[]{:S(2)}, u32[]{:S(2)}) collective-permute-start(f32[4,64,256]{1,0,2:T(4,128)S(1)} %get-tuple-element.311), channel_id=1, source_target_pairs={{0,1},{1,2},{2,3},{3,4},{4,5},{5,6},{6,7},{7,8},{8,9},{9,10},{10,1... | collective-permute-start | bytes 786440 | tf_op jit(solution)/shard_map/while/body/eval_jaxpr/ppermute | solution.py:16
  644.3 15.6 %collective-permute-start.1 = (f32[4,64,256]{1,0,2:T(4,128)S(1)}, f32[4,64,256]{1,0,2:T(4,128)S(1)}, u32[]{:S(2)}, u32[]{:S(2)}) collective-permute-start(f32[4,64,256]{1,0,2:T(4,128)S(1)} %get-tuple-element.312), channel_id=1, source_target_pairs={{1,0},{2,1},{3,2},{4,3},{5,4},{6,5},{7,6},{8,7},{9,8},{10,9},{11,1... | collective-permute-start | bytes 786440 | tf_op jit(solution)/shard_map/while/body/eval_jaxpr/ppermute | solution.py:17
  645.6 16.5 %collective-permute-start = (f32[4,64,256]{1,0,2:T(4,128)S(1)}, f32[4,64,256]{1,0,2:T(4,128)}, u32[]{:S(2)}, u32[]{:S(2)}) collective-permute-start(f32[4,64,256]{1,0,2:T(4,128)S(1)} %get-tuple-element.311), channel_id=1, source_target_pairs={{0,1},{1,2},{2,3},{3,4},{4,5},{5,6},{6,7},{7,8},{8,9},{9,10},{10,1... | collective-permute-start | bytes 786440 | tf_op jit(solution)/shard_map/while/body/eval_jaxpr/ppermute | solution.py:16
  681.1 13.4 %collective-permute-start.1 = (f32[4,64,256]{1,0,2:T(4,128)S(1)}, f32[4,64,256]{1,0,2:T(4,128)S(1)}, u32[]{:S(2)}, u32[]{:S(2)}) collective-permute-start(f32[4,64,256]{1,0,2:T(4,128)S(1)} %get-tuple-element.312), channel_id=1, source_target_pairs={{1,0},{2,1},{3,2},{4,3},{5,4},{6,5},{7,6},{8,7},{9,8},{10,9},{11,1... | collective-permute-start | bytes 786440 | tf_op jit(solution)/shard_map/while/body/eval_jaxpr/ppermute | solution.py:17
  682.4 14.2 %collective-permute-start = (f32[4,64,256]{1,0,2:T(4,128)S(1)}, f32[4,64,256]{1,0,2:T(4,128)}, u32[]{:S(2)}, u32[]{:S(2)}) collective-permute-start(f32[4,64,256]{1,0,2:T(4,128)S(1)} %get-tuple-element.311), channel_id=1, source_target_pairs={{0,1},{1,2},{2,3},{3,4},{4,5},{5,6},{6,7},{7,8},{8,9},{9,10},{10,1... | collective-permute-start | bytes 786440 | tf_op jit(solution)/shard_map/while/body/eval_jaxpr/ppermute | solution.py:16
  (64 other events, 665.2 us)
Sparse Core Ops, SparseCore 0:
  717.9 109.4 reduce-scatter.1
